TPU v7x, 32 devices: a whole 2x2x4 slice. The times are simulated.
32 devices in a mesh: mesh: 8 (over y, x, core), state: 4 (over z).
Axes of the slice: x: 2, y: 2, z: 4, core: 2. Of those that a mesh axis runs over, the one named last changes fastest.
Arguments:
- kern_blocks: bfloat16 [192, 16, 128, 128], P('mesh'), may hold values from 4.296875e-06 to 0.13744531
- kern_cols: int32 [192, 16], P('mesh'), may hold values from 0 to 191, as said below
- state_kernel: bfloat16 [512, 512], replicated, may hold values from 0 to 0.61, as said below
- start_v: float32 [24576, 512], P('mesh', 'state'), may hold values from 0.5 to 5
- mu: float32 [24576, 512], P(('mesh', 'state')), may hold values from 0.2 to 2
- nu: float32 [24576, 512], P('mesh', 'state'), may hold values from 0.2 to 2
Outputs:
- potential_u: float32 [24576, 512], P(('mesh', 'state'))
- potential_v: float32 [24576, 512], P('mesh', 'state')
Inputs may be any that keep to these rules, and one draw needn't show every extreme that they name: `kern_cols`: each block row names 16 different block columns, its own block among them. The block rows held by index d of mesh (rows d * 24 to (d + 1) * 24 - 1) refer, among the blocks of index d - 1 and d + 1 (wrapping around 8), only to the last 6 blocks of d - 1 and the first 6 blocks of d + 1, and to all of them; among the blocks of every other index, to at most 2 distinct blocks, and to exactly 2 of index d + 2. How many other indices they reach differs from index to index. `state_kernel`: each row has a positive diagonal entry.
All inputs are finite; a program needn't handle non-finite values.
Results may differ from a plain program's by a relative error of at most 0.0033.
Values may be sent and summed in bfloat16 or wider, within the bound.
No kernel may reach another device: no remote copies, remote signals or barrier semaphores. Data moves between devices by JAX's collectives and lax.ppermute only.
A program may use at most 192 MiB of HBM per device.

v0:
```python
import jax
import jax.numpy as jnp
from jax import lax
from jax.sharding import PartitionSpec as P

CAP_FAR = 2
ITERS = 2
CAP_NEAR = 6


def padded_2(cells, sides, width):
    for axis, dim in sides:
        count = lax.axis_size(axis)
        head = lax.slice_in_dim(cells, 0, width, axis=dim)
        tail = lax.slice_in_dim(cells, cells.shape[dim] - width, cells.shape[dim], axis=dim)
        cells = jnp.concatenate(
            [
                lax.ppermute(tail, axis, [(i, (i + 1) % count) for i in range(count)]),
                cells,
                lax.ppermute(head, axis, [((i + 1) % count, i) for i in range(count)]),
            ],
            axis=dim,
        )
    return cells


def shifted(value, axis, steps):
    count = lax.axis_size(axis)
    pairs = [(source, (source + steps) % count) for source in range(count)]
    return lax.ppermute(value, axis, pairs)


def request_plan(owners, places, remote, peer_count, block_rows, width):
    peer_ids = jnp.arange(peer_count, dtype=jnp.int32)
    place_ids = jnp.arange(block_rows, dtype=jnp.int32)
    matches = (
        remote[:, None, None]
        & (owners[:, None, None] == peer_ids[None, :, None])
        & (places[:, None, None] == place_ids[None, None, :])
    )
    matches = matches.astype(jnp.int32)
    needed = jnp.max(matches, axis=0)
    ranking = jnp.cumsum(needed, axis=1) - needed
    ref_slots = jnp.sum(matches * ranking[None, :, :], axis=(1, 2))
    slot_ids = jnp.arange(width, dtype=jnp.int32)
    selected = needed[:, :, None] * (ranking[:, :, None] == slot_ids[None, None, :]).astype(
        jnp.int32
    )
    requests = jnp.sum(selected * place_ids[None, :, None], axis=1)
    return (ref_slots, requests)


def rounded_sum(values):
    return lax.optimization_barrier(values.astype(jnp.bfloat16)).astype(jnp.float32)


def per_device(kern_blocks, kern_cols, state_kernel, start_v, mu, nu):
    block_rows, degree, block_size, _ = kern_blocks.shape
    local_rows, state_cols = start_v.shape
    peer_count = lax.axis_size("mesh")
    state_count = lax.axis_size("state")
    my_index = lax.axis_index("mesh")
    left_index = (my_index + peer_count - 1) % peer_count
    right_index = (my_index + 1) % peer_count
    flat_cols = kern_cols.reshape(-1)
    owners = flat_cols // block_rows
    places = flat_cols % block_rows
    near_width = CAP_NEAR
    far_base = block_rows + 2 * near_width
    remote = (owners != my_index) & (owners != left_index) & (owners != right_index)
    ref_slots, requests = request_plan(owners, places, remote, peer_count, block_rows, CAP_FAR)
    asked = lax.all_to_all(requests, "mesh", split_axis=0, concat_axis=0, tiled=True)
    near_source = jnp.where(
        owners == left_index,
        places - (block_rows - near_width),
        jnp.where(owners == right_index, near_width + block_rows + places, near_width + places),
    )
    sources = jnp.where(remote, far_base + owners * CAP_FAR + ref_slots, near_source)
    table_size = far_base + peer_count * CAP_FAR
    flat_asked = asked.reshape(-1)
    values = start_v
    potential_u = mu
    for sweep in range(ITERS):
        rounded_v = values.astype(jnp.bfloat16)
        blocks = rounded_v.reshape(block_rows, block_size, state_cols)
        padded = padded_2(rounded_v, (("mesh", 0),), near_width * block_size)
        incoming = lax.all_to_all(blocks[asked], "mesh", split_axis=0, concat_axis=0, tiled=True)
        table = jnp.concatenate(
            [
                padded.reshape(-1, block_size, state_cols),
                incoming.reshape(-1, block_size, state_cols),
            ],
            axis=0,
        )
        picked = table[sources].reshape(block_rows, degree, block_size, state_cols)
        applied = jnp.einsum(
            "rkab,rkbc->rac", kern_blocks, picked, preferred_element_type=jnp.float32
        )
        pieces = applied.astype(jnp.bfloat16).reshape(
            state_count, local_rows // state_count, state_cols
        )
        mixed = jnp.einsum(
            "xrl,jl->xrj",
            lax.all_to_all(pieces, "state", split_axis=0, concat_axis=2, tiled=True),
            state_kernel,
            preferred_element_type=jnp.float32,
        )
        potential_u = mu / mixed[0]
        back_rows = jnp.dot(
            potential_u.astype(jnp.bfloat16), state_kernel, preferred_element_type=jnp.float32
        ).astype(jnp.bfloat16)
        returned = lax.all_to_all(back_rows, "state", split_axis=1, concat_axis=0, tiled=True)
        returned = returned.reshape(block_rows, block_size, state_cols)
        spread = jnp.einsum(
            "rkab,rac->rkbc", kern_blocks, returned, preferred_element_type=jnp.float32
        )
        contrib_table = jax.ops.segment_sum(
            spread.reshape(-1, block_size, state_cols), sources, num_segments=table_size
        )
        own_part = rounded_sum(contrib_table[near_width : near_width + block_rows])
        to_left = contrib_table[:near_width].astype(jnp.bfloat16)
        to_right = contrib_table[near_width + block_rows : far_base].astype(jnp.bfloat16)
        from_right = shifted(to_left, "mesh", -1)
        from_left = shifted(to_right, "mesh", 1)
        outgoing = (
            contrib_table[far_base:]
            .reshape(peer_count, CAP_FAR, block_size, state_cols)
            .astype(jnp.bfloat16)
        )
        arriving = lax.all_to_all(outgoing, "mesh", split_axis=0, concat_axis=0, tiled=True)
        arriving = arriving.reshape(-1, block_size, state_cols).astype(jnp.float32)
        totals = own_part + jax.ops.segment_sum(arriving, flat_asked, num_segments=block_rows)
        totals = totals.at[:near_width].add(from_left.astype(jnp.float32))
        totals = totals.at[block_rows - near_width :].add(from_right.astype(jnp.float32))
        values = nu / totals.reshape(local_rows, state_cols)
    return (potential_u, values)


def solution(mesh):
    placed = (
        P("mesh", None, None, None),
        P("mesh", None),
        P(),
        P("mesh", "state"),
        P(("mesh", "state"), None),
        P("mesh", "state"),
    )
    return jax.shard_map(
        per_device,
        mesh=mesh,
        in_specs=placed,
        out_specs=(P(("mesh", "state"), None), P("mesh", "state")),
        check_vma=False,
    )
```

profile of v0, /device:TPU:0, one launch (start us, length us, event | category | flops | bytes accessed | tf_op | source)
XLA Modules:
  0.0 483.5 jit_solution(15671120138899974268)
XLA Ops:
  3.9 5.2 %all-to-all-start = ((s32[8,1,2]{2,1,0:T(1,128)}), s32[8,1,2]{2,1,0:T(1,128)S(1)}, u32[]{:S(2)}, u32[]{:S(2)}) async-start(s32[8,1,2]{2,1,0:T(1,128)} %copy.49), calls=%async_computation | async-start | bytes 8192 | tf_op jit(solution)/shard_map/all_to_all | solution.py:72
  11.2 2.2 collective-permute-start.1
  15.5 3.5 all-to-all-start.1
  19.1 9.5 %all-to-all-done.1 = bf16[8,2,128,128]{3,2,1,0:T(8,128)(2,1)S(1)} async-done(((bf16[8,2,128,128]{3,2,1,0:T(8,128)(2,1)}), bf16[8,2,128,128]{3,2,1,0:T(8,128)(2,1)S(1)}, u32[]{:S(2)}, u32[]{:S(2)}) %all-to-all-start.1) | async-done | bytes 524320 | tf_op jit(solution)/shard_map/all_to_all | solution.py:87
  30.7 11.3 %gather_fusion.1 = bf16[384,128,128]{2,1,0:T(8,128)(2,1)} fusion(bf16[52,128,128]{2,1,0:T(8,128)(2,1)S(1)} %pad_maximum_fusion, s32[1024]{0:T(1024)S(1)} %pad_clamp_fusion), kind=kCustom, calls=%fused_computation.1 | custom fusion | bytes 25167360 | tf_op jit(solution)/shard_map/gather | solution.py:95
  42.0 11.6 %bitcast_convert_fusion.1 = bf16[24,128,128]{1,2,0:T(8,128)(2,1)S(1)} fusion(bf16[24,16,128,128]{3,2,1,0:T(8,128)(2,1)} %param.14, bf16[24,16,128,128]{3,2,1,0:T(8,128)(2,1)} %bitcast.90), kind=kOutput, calls=%fused_computation.14 | convolution fusion | flops 1611005952 | bytes 25952256 | tf_op jit(solution)/shard_map/rkab,rkbc->rac/dot_general | solution.py:96
  53.8 22.5 %all_to_all.94 = bf16[4,768,128]{1,2,0:T(8,128)(2,1)S(1)} all-to-all(bf16[4,768,128]{1,2,0:T(8,128)(2,1)S(1)} %copy.52), channel_id=1, replica_groups=mesh['mesh'=8,'state'=4] {'state'}, dimensions={0} | all-to-all | bytes 1572864 | tf_op jit(solution)/shard_map/all_to_all | solution.py:104
  76.4 2.4 convolution_convert_fusion.1
  79.2 21.5 %all_to_all.95 = bf16[768,4,128]{2,0,1:T(8,128)(2,1)S(1)} all-to-all(bf16[768,4,128]{2,0,1:T(8,128)(2,1)S(1)} %copy.53), channel_id=1, replica_groups=mesh['mesh'=8,'state'=4] {'state'}, dimensions={1} | all-to-all | bytes 1572864 | tf_op jit(solution)/shard_map/all_to_all | solution.py:112
  100.7 16.3 %fusion.14 = f32[24,128,16,128]{3,1,2,0:T(8,128)} fusion(bf16[24,128,128,1]{2,1,3,0:T(8,128)(2,1)S(1)} %bitcast.95, bf16[24,16,128,128]{3,2,1,0:T(8,128)(2,1)} %param.14), kind=kOutput, calls=%fused_computation.62 | convolution fusion | flops 1610612736 | bytes 38535168 | tf_op jit(solution)/shard_map/rkab,rac->rkbc/dot_general | solution.py:114
  117.1 24.7 %copy.55 = f32[384,128,128]{2,1,0:T(8,128)} copy(f32[384,128,128]{1,2,0:T(8,128)} %bitcast.87) | data formatting | bytes 50331648 | tf_op jit(solution)/shard_map/reshape | solution.py:118
  141.7 2.2 broadcast.426.clone
  144.0 79.5 %scatter_fusion = f32[52,128,128]{2,1,0:T(8,128)} fusion(f32[52,128,128]{2,1,0:T(8,128)} %broadcast.426.clone, s32[384]{0:T(512)S(1)} %get-tuple-element.51, f32[384,128,128]{2,1,0:T(8,128)} %copy.55), kind=kCustom, calls=%fused_computation.4 | custom fusion | flops 6291456 | bytes 75499008 | tf_op jit(solution)/shard_map/scatter-add | solution.py:117
  223.5 2.2 convert.14
  226.6 5.2 %all-to-all-start.4 = ((bf16[8,2,128,128]{3,2,1,0:T(8,128)(2,1)}), bf16[8,2,128,128]{3,2,1,0:T(8,128)(2,1)}, u32[]{:S(2)}, u32[]{:S(2)}) async-start(bf16[8,2,128,128]{3,2,1,0:T(8,128)(2,1)} %bitcast.20), calls=%async_computation.4 | async-start | bytes 1048576 | tf_op jit(solution)/shard_map/all_to_all | solution.py:130
  234.9 2.2 collective-permute-start.3
  237.1 5.1 %all-to-all-done.4 = bf16[8,2,128,128]{3,2,1,0:T(8,128)(2,1)} async-done(((bf16[8,2,128,128]{3,2,1,0:T(8,128)(2,1)}), bf16[8,2,128,128]{3,2,1,0:T(8,128)(2,1)}, u32[]{:S(2)}, u32[]{:S(2)}) %all-to-all-start.4) | async-done | bytes 524320 | tf_op jit(solution)/shard_map/all_to_all | solution.py:130
  247.8 2.6 collective-permute-start.5
  251.9 3.7 all-to-all-start.5
  257.0 8.0 %all-to-all-done.5 = bf16[8,2,128,128]{3,2,1,0:T(8,128)(2,1)S(1)} async-done(((bf16[8,2,128,128]{3,2,1,0:T(8,128)(2,1)}), bf16[8,2,128,128]{3,2,1,0:T(8,128)(2,1)S(1)}, u32[]{:S(2)}, u32[]{:S(2)}) %all-to-all-start.5) | async-done | bytes 524320 | tf_op jit(solution)/shard_map/all_to_all | solution.py:87
  266.5 11.3 %gather_fusion.3 = bf16[384,128,128]{2,1,0:T(8,128)(2,1)} fusion(bf16[52,128,128]{2,1,0:T(8,128)(2,1)S(1)} %pad_maximum_fusion.1, s32[1024]{0:T(1024)S(1)} %pad_clamp_fusion), kind=kCustom, calls=%fused_computation.3 | custom fusion | bytes 25167360 | tf_op jit(solution)/shard_map/gather | solution.py:95
  277.8 11.6 %bitcast_convert_fusion = bf16[24,128,128]{1,2,0:T(8,128)(2,1)S(1)} fusion(bf16[24,16,128,128]{3,2,1,0:T(8,128)(2,1)} %param.14, bf16[24,16,128,128]{3,2,1,0:T(8,128)(2,1)} %bitcast.89), kind=kOutput, calls=%fused_computation.11 | convolution fusion | flops 1611005952 | bytes 25952256 | tf_op jit(solution)/shard_map/rkab,rkbc->rac/dot_general | solution.py:96
  289.6 20.5 %all_to_all.96 = bf16[4,768,128]{1,2,0:T(8,128)(2,1)S(1)} all-to-all(bf16[4,768,128]{1,2,0:T(8,128)(2,1)S(1)} %copy.56), channel_id=1, replica_groups=mesh['mesh'=8,'state'=4] {'state'}, dimensions={0} | all-to-all | bytes 1572864 | tf_op jit(solution)/shard_map/all_to_all | solution.py:104
  313.8 21.5 %all_to_all.97 = bf16[768,4,128]{2,0,1:T(8,128)(2,1)S(1)} all-to-all(bf16[768,4,128]{2,0,1:T(8,128)(2,1)S(1)} %copy.57), channel_id=1, replica_groups=mesh['mesh'=8,'state'=4] {'state'}, dimensions={1} | all-to-all | bytes 1572864 | tf_op jit(solution)/shard_map/all_to_all | solution.py:112
  335.3 16.3 %fusion.15 = f32[24,128,16,128]{3,1,2,0:T(8,128)} fusion(bf16[24,128,128,1]{2,1,3,0:T(8,128)(2,1)S(1)} %bitcast.96, bf16[24,16,128,128]{3,2,1,0:T(8,128)(2,1)} %param.14), kind=kOutput, calls=%fused_computation.63 | convolution fusion | flops 1610612736 | bytes 38535168 | tf_op jit(solution)/shard_map/rkab,rac->rkbc/dot_general | solution.py:114
  351.6 24.7 %copy.59 = f32[384,128,128]{2,1,0:T(8,128)} copy(f32[384,128,128]{1,2,0:T(8,128)} %bitcast.88) | data formatting | bytes 50331648 | tf_op jit(solution)/shard_map/reshape | solution.py:118
  376.3 2.2 broadcast.426
  378.5 79.5 %scatter_fusion.2 = f32[52,128,128]{2,1,0:T(8,128)} fusion(f32[52,128,128]{2,1,0:T(8,128)} %broadcast.426, s32[384]{0:T(512)S(1)} %get-tuple-element.51, f32[384,128,128]{2,1,0:T(8,128)} %copy.59), kind=kCustom, calls=%fused_computation.6 | custom fusion | flops 6291456 | bytes 75499008 | tf_op jit(solution)/shard_map/scatter-add | solution.py:117
  458.0 2.2 convert.15
  461.1 5.2 %all-to-all-start.8 = ((bf16[8,2,128,128]{3,2,1,0:T(8,128)(2,1)}), bf16[8,2,128,128]{3,2,1,0:T(8,128)(2,1)}, u32[]{:S(2)}, u32[]{:S(2)}) async-start(bf16[8,2,128,128]{3,2,1,0:T(8,128)(2,1)} %bitcast.41), calls=%async_computation.8 | async-start | bytes 1048576 | tf_op jit(solution)/shard_map/all_to_all | solution.py:130
  468.2 2.2 collective-permute-start.7
  470.4 6.3 %all-to-all-done.8 = bf16[8,2,128,128]{3,2,1,0:T(8,128)(2,1)} async-done(((bf16[8,2,128,128]{3,2,1,0:T(8,128)(2,1)}), bf16[8,2,128,128]{3,2,1,0:T(8,128)(2,1)}, u32[]{:S(2)}, u32[]{:S(2)}) %all-to-all-start.8) | async-done | bytes 524320 | tf_op jit(solution)/shard_map/all_to_all | solution.py:130
  (91 shorter events, 37.1 us)
Async XLA Ops:
  0.6 75.8 %copy-start = (bf16[512,512]{1,0:T(8,128)(2,1)S(1)}, bf16[512,512]{1,0:T(8,128)(2,1)}, u32[]{:S(2)}) copy-start(bf16[512,512]{1,0:T(8,128)(2,1)} %param.16) | copy-start | bytes 1572868
  3.9 9.9 %all-to-all-start = ((s32[8,1,2]{2,1,0:T(1,128)}), s32[8,1,2]{2,1,0:T(1,128)S(1)}, u32[]{:S(2)}, u32[]{:S(2)}) async-start(s32[8,1,2]{2,1,0:T(1,128)} %copy.49), calls=%async_computation | async-start | bytes 8192 | tf_op jit(solution)/shard_map/all_to_all | solution.py:72
  10.7 8.4 %collective-permute-start = (bf16[768,128]{1,0:T(8,128)(2,1)S(1)}, bf16[768,128]{1,0:T(8,128)(2,1)S(1)}, u32[]{:S(2)}, u32[]{:S(2)}) collective-permute-start(bf16[768,128]{1,0:T(8,128)(2,1)S(1)} %get-tuple-element.60), channel_id=1, source_target_pairs={{0,4},{4,8},{8,12},{12,16},{16,20},{20,24},{24,28},{28,0},{1,5},{5... | collective-permute-start | bytes 589832 | tf_op jit(solution)/shard_map/ppermute | solution.py:18
  11.2 7.8 %collective-permute-start.1 = (bf16[768,128]{1,0:T(8,128)(2,1)S(1)}, bf16[768,128]{1,0:T(8,128)(2,1)S(1)}, u32[]{:S(2)}, u32[]{:S(2)}) collective-permute-start(bf16[768,128]{1,0:T(8,128)(2,1)S(1)} %get-tuple-element.61), channel_id=1, source_target_pairs={{4,0},{8,4},{12,8},{16,12},{20,16},{24,20},{28,24},{0,28},{5,1},{9... | collective-permute-start | bytes 589832 | tf_op jit(solution)/shard_map/ppermute | solution.py:20
  15.5 13.2 %all-to-all-start.1 = ((bf16[8,2,128,128]{3,2,1,0:T(8,128)(2,1)}), bf16[8,2,128,128]{3,2,1,0:T(8,128)(2,1)S(1)}, u32[]{:S(2)}, u32[]{:S(2)}) async-start(bf16[8,2,128,128]{3,2,1,0:T(8,128)(2,1)} %bitcast.4), calls=%async_computation.1 | async-start | bytes 1048576 | tf_op jit(solution)/shard_map/all_to_all | solution.py:87
  28.7 0.8 copy-start.5
  225.7 7.3 %copy-start.1 = (bf16[52,128,128]{2,1,0:T(8,128)(2,1)}, bf16[52,128,128]{2,1,0:T(8,128)(2,1)S(1)}, u32[]{:S(2)}) copy-start(bf16[52,128,128]{2,1,0:T(8,128)(2,1)S(1)} %convert.14) | copy-start | bytes 5111812
  226.6 15.6 %all-to-all-start.4 = ((bf16[8,2,128,128]{3,2,1,0:T(8,128)(2,1)}), bf16[8,2,128,128]{3,2,1,0:T(8,128)(2,1)}, u32[]{:S(2)}, u32[]{:S(2)}) async-start(bf16[8,2,128,128]{3,2,1,0:T(8,128)(2,1)} %bitcast.20), calls=%async_computation.4 | async-start | bytes 1048576 | tf_op jit(solution)/shard_map/all_to_all | solution.py:130
  234.4 10.9 %collective-permute-start.2 = (bf16[6,128,128]{2,1,0:T(8,128)(2,1)S(1)}, bf16[6,128,128]{2,1,0:T(8,128)(2,1)}, u32[]{:S(2)}, u32[]{:S(2)}) collective-permute-start(bf16[6,128,128]{2,1,0:T(8,128)(2,1)S(1)} %get-tuple-element.57), channel_id=1, source_target_pairs={{0,4},{4,8},{8,12},{12,16},{16,20},{20,24},{24,28},{28,0},{1,5},{5... | collective-permute-start | bytes 589832 | tf_op jit(solution)/shard_map/ppermute | solution.py:30
  234.9 11.5 %collective-permute-start.3 = (bf16[6,128,128]{2,1,0:T(8,128)(2,1)S(1)}, bf16[6,128,128]{2,1,0:T(8,128)(2,1)}, u32[]{:S(2)}, u32[]{:S(2)}) collective-permute-start(bf16[6,128,128]{2,1,0:T(8,128)(2,1)S(1)} %get-tuple-element.56), channel_id=1, source_target_pairs={{0,28},{4,0},{8,4},{12,8},{16,12},{20,16},{24,20},{28,24},{1,29},{... | collective-permute-start | bytes 589832 | tf_op jit(solution)/shard_map/ppermute | solution.py:30
  244.9 2.5 copy-start.3
  247.8 8.1 %collective-permute-start.4 = (bf16[768,128]{1,0:T(8,128)(2,1)S(1)}, bf16[768,128]{1,0:T(8,128)(2,1)S(1)}, u32[]{:S(2)}, u32[]{:S(2)}) collective-permute-start(bf16[768,128]{1,0:T(8,128)(2,1)S(1)} %get-tuple-element.58), channel_id=1, source_target_pairs={{0,4},{4,8},{8,12},{12,16},{16,20},{20,24},{24,28},{28,0},{1,5},{5... | collective-permute-start | bytes 589832 | tf_op jit(solution)/shard_map/ppermute | solution.py:18
  247.8 8.0 %collective-permute-start.5 = (bf16[768,128]{1,0:T(8,128)(2,1)S(1)}, bf16[768,128]{1,0:T(8,128)(2,1)S(1)}, u32[]{:S(2)}, u32[]{:S(2)}) collective-permute-start(bf16[768,128]{1,0:T(8,128)(2,1)S(1)} %get-tuple-element.59), channel_id=1, source_target_pairs={{4,0},{8,4},{12,8},{16,12},{20,16},{24,20},{28,24},{0,28},{5,1},{9... | collective-permute-start | bytes 589832 | tf_op jit(solution)/shard_map/ppermute | solution.py:20
  251.9 13.2 %all-to-all-start.5 = ((bf16[8,2,128,128]{3,2,1,0:T(8,128)(2,1)}), bf16[8,2,128,128]{3,2,1,0:T(8,128)(2,1)S(1)}, u32[]{:S(2)}, u32[]{:S(2)}) async-start(bf16[8,2,128,128]{3,2,1,0:T(8,128)(2,1)} %bitcast.25), calls=%async_computation.5 | async-start | bytes 1048576 | tf_op jit(solution)/shard_map/all_to_all | solution.py:87
  312.2 1.1 copy-start.6
  460.3 6.1 %copy-start.2 = (bf16[52,128,128]{2,1,0:T(8,128)(2,1)}, bf16[52,128,128]{2,1,0:T(8,128)(2,1)S(1)}, u32[]{:S(2)}) copy-start(bf16[52,128,128]{2,1,0:T(8,128)(2,1)S(1)} %convert.15) | copy-start | bytes 5111812
  461.1 15.6 %all-to-all-start.8 = ((bf16[8,2,128,128]{3,2,1,0:T(8,128)(2,1)}), bf16[8,2,128,128]{3,2,1,0:T(8,128)(2,1)}, u32[]{:S(2)}, u32[]{:S(2)}) async-start(bf16[8,2,128,128]{3,2,1,0:T(8,128)(2,1)} %bitcast.41), calls=%async_computation.8 | async-start | bytes 1048576 | tf_op jit(solution)/shard_map/all_to_all | solution.py:130
  467.6 12.2 %collective-permute-start.6 = (bf16[6,128,128]{2,1,0:T(8,128)(2,1)S(1)}, bf16[6,128,128]{2,1,0:T(8,128)(2,1)}, u32[]{:S(2)}, u32[]{:S(2)}) collective-permute-start(bf16[6,128,128]{2,1,0:T(8,128)(2,1)S(1)} %get-tuple-element.55), channel_id=1, source_target_pairs={{0,4},{4,8},{8,12},{12,16},{16,20},{20,24},{24,28},{28,0},{1,5},{5... | collective-permute-start | bytes 589832 | tf_op jit(solution)/shard_map/ppermute | solution.py:30
  468.2 12.8 %collective-permute-start.7 = (bf16[6,128,128]{2,1,0:T(8,128)(2,1)S(1)}, bf16[6,128,128]{2,1,0:T(8,128)(2,1)}, u32[]{:S(2)}, u32[]{:S(2)}) collective-permute-start(bf16[6,128,128]{2,1,0:T(8,128)(2,1)S(1)} %get-tuple-element.54), channel_id=1, source_target_pairs={{0,28},{4,0},{8,4},{12,8},{16,12},{20,16},{24,20},{28,24},{1,29},{... | collective-permute-start | bytes 589832 | tf_op jit(solution)/shard_map/ppermute | solution.py:30
  479.5 2.5 copy-start.4
where the time goes:
time: 487 us; the launch traced here: 484 us
  other arithmetic  184 us (38%)
  local copies, waits for them, and re-layouts  88.1 us (18%)
  blocking collectives  86.1 us (18%)
  matrix products  61 us (13%)
  starting transfers between devices  33.8 us (7%)
  waiting for transfers between devices  29.9 us (6%)
    scatter-add x2, other arithmetic, per_device(): jax.ops.segment_sum(spread.reshape(-1, block_size, state_cols), sources,...  159 us
    reshape x2, local copies, waits for them, and re-layouts, per_device(): spread.reshape(-1, block_size, state_cols)  49.3 us
    all_to_all x2, blocking collectives, per_device(): lax.all_to_all(pieces, 'state', split_axis=0, concat_axis=2, tiled=True)  43.1 us
    all_to_all x2, blocking collectives, per_device(): lax.all_to_all(back_rows, 'state', split_axis=1, concat_axis=0, tiled=True)  43 us
    dot_general x2, matrix products, per_device(): jnp.einsum('rkab,rac->rkbc', kern_blocks, returned, preferred_element_typ...  32.7 us
    dot_general x2, matrix products, per_device(): jnp.einsum('rkab,rkbc->rac', kern_blocks, picked, preferred_element_type=...  23.2 us
    gather x2, local copies, waits for them, and re-layouts, per_device(): picked = table[sources].reshape(block_rows, degree, block_size, state_cols)  22.6 us
    all_to_all x2, waiting for transfers between devices, per_device(): lax.all_to_all(blocks[asked], 'mesh', split_axis=0, concat_axis=0, tiled=...  17.6 us
  transfers between devices with their start and end apart: 13, of which 7 were waited for; matrix products, arithmetic and copies ran while one was open for 4% of the time, Pallas kernels for 0%

commit v1 on v0

--- a/solution.py
+++ b/solution.py
@@ -1,3 +1,4 @@
+import functools
 import jax
 import jax.numpy as jnp
 from jax import lax
@@ -6,6 +7,21 @@
 CAP_FAR = 2
 ITERS = 2
 CAP_NEAR = 6
+
+
+def draw_sources_all(slab_in, along_axis):
+    return jnp.concatenate(
+        lax.all_to_all(
+            jnp.stack(jnp.split(slab_in, lax.axis_size(along_axis), axis=1), axis=0),
+            along_axis,
+            0,
+            0,
+        ),
+        axis=0,
+    )
+
+
+put_sectors = functools.partial(draw_sources_all, along_axis="state")
 
 
 def padded_2(cells, sides, width):
@@ -109,7 +125,7 @@
         back_rows = jnp.dot(
             potential_u.astype(jnp.bfloat16), state_kernel, preferred_element_type=jnp.float32
         ).astype(jnp.bfloat16)
-        returned = lax.all_to_all(back_rows, "state", split_axis=1, concat_axis=0, tiled=True)
+        returned = put_sectors(back_rows)
         returned = returned.reshape(block_rows, block_size, state_cols)
         spread = jnp.einsum(
             "rkab,rac->rkbc", kern_blocks, returned, preferred_element_type=jnp.float32

time: 487 us -> 486 us (level)
  no operation moved by 1% of the time
where the time goes in v1:
time: 486 us; the launch traced here: 482 us
  other arithmetic  184 us (38%)
  local copies, waits for them, and re-layouts  87.5 us (18%)
  blocking collectives  86.1 us (18%)
  matrix products  60.9 us (13%)
  starting transfers between devices  33 us (7%)
  waiting for transfers between devices  29.9 us (6%)
    scatter-add x2, other arithmetic, per_device(): jax.ops.segment_sum(spread.reshape(-1, block_size, state_cols), sources,...  159 us
    reshape x2, local copies, waits for them, and re-layouts, per_device(): spread.reshape(-1, block_size, state_cols)  49.3 us
    all_to_all x2, blocking collectives, per_device(): lax.all_to_all(pieces, 'state', split_axis=0, concat_axis=2, tiled=True)  43.1 us
    all_to_all x2, blocking collectives, draw_sources_all(): lax.all_to_all(jnp.stack(jnp.split(slab_in, lax.axis_size(along_axis), ax...  43 us
    dot_general x2, matrix products, per_device(): jnp.einsum('rkab,rac->rkbc', kern_blocks, returned, preferred_element_typ...  32.7 us
    dot_general x2, matrix products, per_device(): jnp.einsum('rkab,rkbc->rac', kern_blocks, picked, preferred_element_type=...  23.2 us
    gather x2, local copies, waits for them, and re-layouts, per_device(): picked = table[sources].reshape(block_rows, degree, block_size, state_cols)  22.6 us
    all_to_all x2, waiting for transfers between devices, per_device(): lax.all_to_all(blocks[asked], 'mesh', split_axis=0, concat_axis=0, tiled=...  17.6 us
  transfers between devices with their start and end apart: 13, of which 7 were waited for; matrix products, arithmetic and copies ran while one was open for 4% of the time, Pallas kernels for 0%

profile of v1, /device:TPU:0, one launch (start us, length us, event | category | flops | bytes accessed | tf_op | source)
XLA Modules:
  0.0 482.5 jit_solution(12345297492549750532)
XLA Ops:
  3.9 5.2 %all-to-all-start = ((s32[8,1,2]{2,1,0:T(1,128)}), s32[8,1,2]{2,1,0:T(1,128)S(1)}, u32[]{:S(2)}, u32[]{:S(2)}) async-start(s32[8,1,2]{2,1,0:T(1,128)} %copy.47), calls=%async_computation | async-start | bytes 8192 | tf_op jit(solution)/shard_map/all_to_all | solution.py:88
  11.2 2.2 collective-permute-start.1
  15.5 3.5 all-to-all-start.1
  19.1 9.5 %all-to-all-done.1 = bf16[8,2,128,128]{3,2,1,0:T(8,128)(2,1)S(1)} async-done(((bf16[8,2,128,128]{3,2,1,0:T(8,128)(2,1)}), bf16[8,2,128,128]{3,2,1,0:T(8,128)(2,1)S(1)}, u32[]{:S(2)}, u32[]{:S(2)}) %all-to-all-start.1) | async-done | bytes 524320 | tf_op jit(solution)/shard_map/all_to_all | solution.py:103
  30.7 11.3 %gather_fusion.1 = bf16[384,128,128]{2,1,0:T(8,128)(2,1)} fusion(bf16[52,128,128]{2,1,0:T(8,128)(2,1)S(1)} %pad_maximum_fusion, s32[1024]{0:T(1024)S(1)} %pad_clamp_fusion), kind=kCustom, calls=%fused_computation.1 | custom fusion | bytes 25167360 | tf_op jit(solution)/shard_map/gather | solution.py:111
  42.0 11.6 %bitcast_convert_fusion.1 = bf16[24,128,128]{1,2,0:T(8,128)(2,1)S(1)} fusion(bf16[24,16,128,128]{3,2,1,0:T(8,128)(2,1)} %param.14, bf16[24,16,128,128]{3,2,1,0:T(8,128)(2,1)} %bitcast.100), kind=kOutput, calls=%fused_computation.14 | convolution fusion | flops 1611005952 | bytes 25952256 | tf_op jit(solution)/shard_map/rkab,rkbc->rac/dot_general | solution.py:112
  53.9 22.5 %all_to_all.72 = bf16[4,768,128]{1,2,0:T(8,128)(2,1)S(1)} all-to-all(bf16[4,768,128]{1,2,0:T(8,128)(2,1)S(1)} %copy.50), channel_id=1, replica_groups=mesh['mesh'=8,'state'=4] {'state'}, dimensions={0} | all-to-all | bytes 1572864 | tf_op jit(solution)/shard_map/all_to_all | solution.py:120
  76.4 2.5 convolution_convert_fusion.1
  79.1 21.5 %all_to_all.73 = bf16[4,768,128]{2,1,0:T(8,128)(2,1)S(1)} all-to-all(bf16[4,768,128]{2,1,0:T(8,128)(2,1)S(1)} %pad_maximum_fusion.4), channel_id=1, replica_groups=mesh['mesh'=8,'state'=4] {'state'}, dimensions={0} | all-to-all | bytes 1572864 | tf_op jit(solution)/shard_map/all_to_all | solution.py:14
  100.6 16.3 %fusion.14 = f32[24,128,16,128]{3,1,2,0:T(8,128)} fusion(bf16[24,128,128,1]{2,1,3,0:T(8,128)(2,1)S(1)} %bitcast.105, bf16[24,16,128,128]{3,2,1,0:T(8,128)(2,1)} %param.14), kind=kOutput, calls=%fused_computation.72 | convolution fusion | flops 1610612736 | bytes 38535168 | tf_op jit(solution)/shard_map/rkab,rac->rkbc/dot_general | solution.py:130
  117.0 24.7 %copy.52 = f32[384,128,128]{2,1,0:T(8,128)} copy(f32[384,128,128]{1,2,0:T(8,128)} %bitcast.97) | data formatting | bytes 50331648 | tf_op jit(solution)/shard_map/reshape | solution.py:134
  141.6 2.2 broadcast.426.clone
  143.8 79.6 %scatter_fusion = f32[52,128,128]{2,1,0:T(8,128)} fusion(f32[52,128,128]{2,1,0:T(8,128)} %broadcast.426.clone, s32[384]{0:T(512)S(1)} %get-tuple-element.51, f32[384,128,128]{2,1,0:T(8,128)} %copy.52), kind=kCustom, calls=%fused_computation.4 | custom fusion | flops 6291456 | bytes 75499008 | tf_op jit(solution)/shard_map/scatter-add | solution.py:133
  223.4 2.2 convert.14
  226.6 4.8 all-to-all-start.4
  234.4 2.2 collective-permute-start.3
  236.6 5.1 %all-to-all-done.4 = bf16[8,2,128,128]{3,2,1,0:T(8,128)(2,1)} async-done(((bf16[8,2,128,128]{3,2,1,0:T(8,128)(2,1)}), bf16[8,2,128,128]{3,2,1,0:T(8,128)(2,1)}, u32[]{:S(2)}, u32[]{:S(2)}) %all-to-all-start.4) | async-done | bytes 524320 | tf_op jit(solution)/shard_map/all_to_all | solution.py:146
  247.4 2.6 collective-permute-start.5
  251.4 3.7 all-to-all-start.5
  256.5 8.0 %all-to-all-done.5 = bf16[8,2,128,128]{3,2,1,0:T(8,128)(2,1)S(1)} async-done(((bf16[8,2,128,128]{3,2,1,0:T(8,128)(2,1)}), bf16[8,2,128,128]{3,2,1,0:T(8,128)(2,1)S(1)}, u32[]{:S(2)}, u32[]{:S(2)}) %all-to-all-start.5) | async-done | bytes 524320 | tf_op jit(solution)/shard_map/all_to_all | solution.py:103
  266.0 11.3 %gather_fusion.3 = bf16[384,128,128]{2,1,0:T(8,128)(2,1)} fusion(bf16[52,128,128]{2,1,0:T(8,128)(2,1)S(1)} %pad_maximum_fusion.1, s32[1024]{0:T(1024)S(1)} %pad_clamp_fusion), kind=kCustom, calls=%fused_computation.3 | custom fusion | bytes 25167360 | tf_op jit(solution)/shard_map/gather | solution.py:111
  277.3 11.6 %bitcast_convert_fusion = bf16[24,128,128]{1,2,0:T(8,128)(2,1)S(1)} fusion(bf16[24,16,128,128]{3,2,1,0:T(8,128)(2,1)} %param.14, bf16[24,16,128,128]{3,2,1,0:T(8,128)(2,1)} %bitcast.99), kind=kOutput, calls=%fused_computation.11 | convolution fusion | flops 1611005952 | bytes 25952256 | tf_op jit(solution)/shard_map/rkab,rkbc->rac/dot_general | solution.py:112
  289.2 20.5 %all_to_all.74 = bf16[4,768,128]{1,2,0:T(8,128)(2,1)S(1)} all-to-all(bf16[4,768,128]{1,2,0:T(8,128)(2,1)S(1)} %copy.53), channel_id=1, replica_groups=mesh['mesh'=8,'state'=4] {'state'}, dimensions={0} | all-to-all | bytes 1572864 | tf_op jit(solution)/shard_map/all_to_all | solution.py:120
  313.0 21.5 %all_to_all.75 = bf16[4,768,128]{2,1,0:T(8,128)(2,1)S(1)} all-to-all(bf16[4,768,128]{2,1,0:T(8,128)(2,1)S(1)} %pad_maximum_fusion.5), channel_id=1, replica_groups=mesh['mesh'=8,'state'=4] {'state'}, dimensions={0} | all-to-all | bytes 1572864 | tf_op jit(solution)/shard_map/all_to_all | solution.py:14
  334.5 16.3 %fusion.15 = f32[24,128,16,128]{3,1,2,0:T(8,128)} fusion(bf16[24,128,128,1]{2,1,3,0:T(8,128)(2,1)S(1)} %bitcast.106, bf16[24,16,128,128]{3,2,1,0:T(8,128)(2,1)} %param.14), kind=kOutput, calls=%fused_computation.73 | convolution fusion | flops 1610612736 | bytes 38535168 | tf_op jit(solution)/shard_map/rkab,rac->rkbc/dot_general | solution.py:130
  350.9 24.7 %copy.55 = f32[384,128,128]{2,1,0:T(8,128)} copy(f32[384,128,128]{1,2,0:T(8,128)} %bitcast.98) | data formatting | bytes 50331648 | tf_op jit(solution)/shard_map/reshape | solution.py:134
  375.5 2.2 broadcast.426
  377.7 79.6 %scatter_fusion.2 = f32[52,128,128]{2,1,0:T(8,128)} fusion(f32[52,128,128]{2,1,0:T(8,128)} %broadcast.426, s32[384]{0:T(512)S(1)} %get-tuple-element.51, f32[384,128,128]{2,1,0:T(8,128)} %copy.55), kind=kCustom, calls=%fused_computation.6 | custom fusion | flops 6291456 | bytes 75499008 | tf_op jit(solution)/shard_map/scatter-add | solution.py:133
  457.3 2.2 convert.15
  460.5 4.9 %all-to-all-start.8 = ((bf16[8,2,128,128]{3,2,1,0:T(8,128)(2,1)}), bf16[8,2,128,128]{3,2,1,0:T(8,128)(2,1)}, u32[]{:S(2)}, u32[]{:S(2)}) async-start(bf16[8,2,128,128]{3,2,1,0:T(8,128)(2,1)} %bitcast.45), calls=%async_computation.8 | async-start | bytes 1048576 | tf_op jit(solution)/shard_map/all_to_all | solution.py:146
  467.2 2.2 collective-permute-start.7
  469.4 6.3 %all-to-all-done.8 = bf16[8,2,128,128]{3,2,1,0:T(8,128)(2,1)} async-done(((bf16[8,2,128,128]{3,2,1,0:T(8,128)(2,1)}), bf16[8,2,128,128]{3,2,1,0:T(8,128)(2,1)}, u32[]{:S(2)}, u32[]{:S(2)}) %all-to-all-start.8) | async-done | bytes 524320 | tf_op jit(solution)/shard_map/all_to_all | solution.py:146
  (93 shorter events, 36.7 us)
Async XLA Ops:
  0.6 75.8 %copy-start = (bf16[512,512]{1,0:T(8,128)(2,1)S(1)}, bf16[512,512]{1,0:T(8,128)(2,1)}, u32[]{:S(2)}) copy-start(bf16[512,512]{1,0:T(8,128)(2,1)} %param.16) | copy-start | bytes 1572868
  3.9 9.9 %all-to-all-start = ((s32[8,1,2]{2,1,0:T(1,128)}), s32[8,1,2]{2,1,0:T(1,128)S(1)}, u32[]{:S(2)}, u32[]{:S(2)}) async-start(s32[8,1,2]{2,1,0:T(1,128)} %copy.47), calls=%async_computation | async-start | bytes 8192 | tf_op jit(solution)/shard_map/all_to_all | solution.py:88
  10.7 8.4 %collective-permute-start = (bf16[768,128]{1,0:T(8,128)(2,1)S(1)}, bf16[768,128]{1,0:T(8,128)(2,1)S(1)}, u32[]{:S(2)}, u32[]{:S(2)}) collective-permute-start(bf16[768,128]{1,0:T(8,128)(2,1)S(1)} %get-tuple-element.68), channel_id=1, source_target_pairs={{0,4},{4,8},{8,12},{12,16},{16,20},{20,24},{24,28},{28,0},{1,5},{5... | collective-permute-start | bytes 589832 | tf_op jit(solution)/shard_map/ppermute | solution.py:34
  11.2 7.8 %collective-permute-start.1 = (bf16[768,128]{1,0:T(8,128)(2,1)S(1)}, bf16[768,128]{1,0:T(8,128)(2,1)S(1)}, u32[]{:S(2)}, u32[]{:S(2)}) collective-permute-start(bf16[768,128]{1,0:T(8,128)(2,1)S(1)} %get-tuple-element.69), channel_id=1, source_target_pairs={{4,0},{8,4},{12,8},{16,12},{20,16},{24,20},{28,24},{0,28},{5,1},{9... | collective-permute-start | bytes 589832 | tf_op jit(solution)/shard_map/ppermute | solution.py:36
  15.5 13.2 %all-to-all-start.1 = ((bf16[8,2,128,128]{3,2,1,0:T(8,128)(2,1)}), bf16[8,2,128,128]{3,2,1,0:T(8,128)(2,1)S(1)}, u32[]{:S(2)}, u32[]{:S(2)}) async-start(bf16[8,2,128,128]{3,2,1,0:T(8,128)(2,1)} %bitcast.4), calls=%async_computation.1 | async-start | bytes 1048576 | tf_op jit(solution)/shard_map/all_to_all | solution.py:103
  28.7 0.8 copy-start.5
  225.7 6.9 %copy-start.1 = (bf16[52,128,128]{2,1,0:T(8,128)(2,1)}, bf16[52,128,128]{2,1,0:T(8,128)(2,1)S(1)}, u32[]{:S(2)}) copy-start(bf16[52,128,128]{2,1,0:T(8,128)(2,1)S(1)} %convert.14) | copy-start | bytes 5111812
  226.6 15.2 %all-to-all-start.4 = ((bf16[8,2,128,128]{3,2,1,0:T(8,128)(2,1)}), bf16[8,2,128,128]{3,2,1,0:T(8,128)(2,1)}, u32[]{:S(2)}, u32[]{:S(2)}) async-start(bf16[8,2,128,128]{3,2,1,0:T(8,128)(2,1)} %bitcast.22), calls=%async_computation.4 | async-start | bytes 1048576 | tf_op jit(solution)/shard_map/all_to_all | solution.py:146
  233.9 10.9 %collective-permute-start.2 = (bf16[6,128,128]{2,1,0:T(8,128)(2,1)S(1)}, bf16[6,128,128]{2,1,0:T(8,128)(2,1)}, u32[]{:S(2)}, u32[]{:S(2)}) collective-permute-start(bf16[6,128,128]{2,1,0:T(8,128)(2,1)S(1)} %get-tuple-element.57), channel_id=1, source_target_pairs={{0,4},{4,8},{8,12},{12,16},{16,20},{20,24},{24,28},{28,0},{1,5},{5... | collective-permute-start | bytes 589832 | tf_op jit(solution)/shard_map/ppermute | solution.py:46
  234.4 11.5 %collective-permute-start.3 = (bf16[6,128,128]{2,1,0:T(8,128)(2,1)S(1)}, bf16[6,128,128]{2,1,0:T(8,128)(2,1)}, u32[]{:S(2)}, u32[]{:S(2)}) collective-permute-start(bf16[6,128,128]{2,1,0:T(8,128)(2,1)S(1)} %get-tuple-element.56), channel_id=1, source_target_pairs={{0,28},{4,0},{8,4},{12,8},{16,12},{20,16},{24,20},{28,24},{1,29},{... | collective-permute-start | bytes 589832 | tf_op jit(solution)/shard_map/ppermute | solution.py:46
  244.5 2.5 copy-start.3
  247.3 8.1 %collective-permute-start.4 = (bf16[768,128]{1,0:T(8,128)(2,1)S(1)}, bf16[768,128]{1,0:T(8,128)(2,1)S(1)}, u32[]{:S(2)}, u32[]{:S(2)}) collective-permute-start(bf16[768,128]{1,0:T(8,128)(2,1)S(1)} %get-tuple-element.62), channel_id=1, source_target_pairs={{0,4},{4,8},{8,12},{12,16},{16,20},{20,24},{24,28},{28,0},{1,5},{5... | collective-permute-start | bytes 589832 | tf_op jit(solution)/shard_map/ppermute | solution.py:34
  247.4 8.0 %collective-permute-start.5 = (bf16[768,128]{1,0:T(8,128)(2,1)S(1)}, bf16[768,128]{1,0:T(8,128)(2,1)S(1)}, u32[]{:S(2)}, u32[]{:S(2)}) collective-permute-start(bf16[768,128]{1,0:T(8,128)(2,1)S(1)} %get-tuple-element.63), channel_id=1, source_target_pairs={{4,0},{8,4},{12,8},{16,12},{20,16},{24,20},{28,24},{0,28},{5,1},{9... | collective-permute-start | bytes 589832 | tf_op jit(solution)/shard_map/ppermute | solution.py:36
  251.4 13.2 %all-to-all-start.5 = ((bf16[8,2,128,128]{3,2,1,0:T(8,128)(2,1)}), bf16[8,2,128,128]{3,2,1,0:T(8,128)(2,1)S(1)}, u32[]{:S(2)}, u32[]{:S(2)}) async-start(bf16[8,2,128,128]{3,2,1,0:T(8,128)(2,1)} %bitcast.27), calls=%async_computation.5 | async-start | bytes 1048576 | tf_op jit(solution)/shard_map/all_to_all | solution.py:103
  311.8 1.1 copy-start.6
  459.6 5.7 %copy-start.2 = (bf16[52,128,128]{2,1,0:T(8,128)(2,1)}, bf16[52,128,128]{2,1,0:T(8,128)(2,1)S(1)}, u32[]{:S(2)}) copy-start(bf16[52,128,128]{2,1,0:T(8,128)(2,1)S(1)} %convert.15) | copy-start | bytes 5111812
  460.5 15.2 %all-to-all-start.8 = ((bf16[8,2,128,128]{3,2,1,0:T(8,128)(2,1)}), bf16[8,2,128,128]{3,2,1,0:T(8,128)(2,1)}, u32[]{:S(2)}, u32[]{:S(2)}) async-start(bf16[8,2,128,128]{3,2,1,0:T(8,128)(2,1)} %bitcast.45), calls=%async_computation.8 | async-start | bytes 1048576 | tf_op jit(solution)/shard_map/all_to_all | solution.py:146
  466.6 12.2 %collective-permute-start.6 = (bf16[6,128,128]{2,1,0:T(8,128)(2,1)S(1)}, bf16[6,128,128]{2,1,0:T(8,128)(2,1)}, u32[]{:S(2)}, u32[]{:S(2)}) collective-permute-start(bf16[6,128,128]{2,1,0:T(8,128)(2,1)S(1)} %get-tuple-element.55), channel_id=1, source_target_pairs={{0,4},{4,8},{8,12},{12,16},{16,20},{20,24},{24,28},{28,0},{1,5},{5... | collective-permute-start | bytes 589832 | tf_op jit(solution)/shard_map/ppermute | solution.py:46
  467.2 12.8 %collective-permute-start.7 = (bf16[6,128,128]{2,1,0:T(8,128)(2,1)S(1)}, bf16[6,128,128]{2,1,0:T(8,128)(2,1)}, u32[]{:S(2)}, u32[]{:S(2)}) collective-permute-start(bf16[6,128,128]{2,1,0:T(8,128)(2,1)S(1)} %get-tuple-element.54), channel_id=1, source_target_pairs={{0,28},{4,0},{8,4},{12,8},{16,12},{20,16},{24,20},{28,24},{1,29},{... | collective-permute-start | bytes 589832 | tf_op jit(solution)/shard_map/ppermute | solution.py:46
  478.5 2.5 copy-start.4
